TPU v7x, 32 devices: a whole 2x2x4 slice. The times are simulated.
32 devices in a mesh: rep: 16 (over z, x, core), shard: 2 (over y).
Axes of the slice: x: 2, y: 2, z: 4, core: 2. Of those that a mesh axis runs over, the one named last changes fastest.
Arguments:
- images: bfloat16 [160, 197, 768], P(('rep', 'shard')), may hold values from -6 to 6
- ln1_gain: bfloat16 [768], P('shard'), may hold values from 0.25 to 1.75
- first_norm_bias: bfloat16 [768], P('shard'), may hold values from -3 to 3
- qkv_weight: bfloat16 [768, 2304], P('shard'), may hold values from -0.21875 to 0.21875
- q_bias: bfloat16 [768], P('shard'), may hold values from -3 to 3
- v_bias: bfloat16 [768], P('shard'), may hold values from -3 to 3
- out_weight: bfloat16 [768, 768], P('shard'), may hold values from -1.75 to 1.75
- out_bias: bfloat16 [768], P('shard'), may hold values from -3 to 3
- ln2_gain: bfloat16 [768], P('shard'), may hold values from 0.25 to 1.75
- second_norm_bias: bfloat16 [768], P('shard'), may hold values from -3 to 3
- up_weight: bfloat16 [768, 3072], P('shard'), may hold values from -0.21875 to 0.21875
- up_bias: bfloat16 [3072], P('shard'), may hold values from -3 to 3
- down_weight: bfloat16 [3072, 768], P('shard'), may hold values from -0.109375 to 0.109375
- down_bias: bfloat16 [768], P('shard'), may hold values from -3 to 3
- cotangent: bfloat16 [160, 197, 768], P(('rep', 'shard')), may hold values from -6 to 6
Outputs:
- result: bfloat16 [160, 197, 768], P(('rep', 'shard'))
- grad_images: bfloat16 [160, 197, 768], P(('rep', 'shard'))
- grad_ln1_gain: float32 [768], P('shard')
- grad_ln1_bias: float32 [768], P('shard')
- grad_qkv_weight: float32 [768, 2304], P('shard')
- grad_q_bias: float32 [768], P('shard')
- grad_v_bias: float32 [768], P('shard')
- grad_out_weight: float32 [768, 768], P('shard')
- grad_out_bias: float32 [768], P('shard')
- grad_ln2_gain: float32 [768], P('shard')
- grad_ln2_bias: float32 [768], P('shard')
- grad_up_weight: float32 [768, 3072], P('shard')
- grad_up_bias: float32 [3072], P('shard')
- grad_down_weight: float32 [3072, 768], P('shard')
- grad_down_bias: float32 [768], P('shard')
All inputs are finite; a program needn't handle non-finite values.
Results may differ from a plain program's by a relative error of at most 0.012.
Values may be sent and summed in bfloat16 or wider, within the bound.
No kernel may reach another device: no remote copies, remote signals or barrier semaphores. Data moves between devices by JAX's collectives and lax.ppermute only.
A program may use at most 256 MiB of HBM per device.

v0:
```python
import jax
import jax.numpy as jnp
from jax import lax
from jax.sharding import PartitionSpec as P

HEADS = 12


def matmul(left, right):
    return jnp.dot(left, right, preferred_element_type=jnp.float32)


def norm_statistics(token_rows):
    row_average = jnp.mean(token_rows, axis=-1, keepdims=True)
    centred = token_rows - row_average
    var = jnp.mean(centred * centred, axis=-1, keepdims=True)
    scale_factor = lax.rsqrt(var + 1e-06)
    return (centred * scale_factor, scale_factor)


def norm_backward(normalized_gradient, standardized_input, scale_factor, norm_gain):
    scaled_rows = normalized_gradient * norm_gain
    return scale_factor * (
        scaled_rows
        - jnp.mean(scaled_rows, axis=-1, keepdims=True)
        - standardized_input * jnp.mean(scaled_rows * standardized_input, axis=-1, keepdims=True)
    )


def gelu_parts(pre):
    cdf = 0.5 * (1.0 + lax.erf(pre * 0.7071067811865476))
    dens = jnp.exp(-0.5 * pre * pre) * 0.3989422804014327
    return (pre * cdf, cdf + pre * dens)


def per_device(
    images,
    ln1_gain,
    first_norm_bias,
    qkv_weight,
    q_bias,
    v_bias,
    out_weight,
    out_bias,
    ln2_gain,
    second_norm_bias,
    up_weight,
    up_bias,
    down_weight,
    down_bias,
    cotangent,
):
    count, seq, width = images.shape
    heads = HEADS
    head = width // heads
    scale = head ** (-0.5)
    single_float = jnp.float32
    brain_float16 = jnp.bfloat16
    attention_complete = (
        lax.all_gather(ln1_gain, "shard", axis=0, tiled=True),
        lax.all_gather(first_norm_bias, "shard", axis=0, tiled=True),
        lax.all_gather(qkv_weight, "shard", axis=0, tiled=True),
        lax.all_gather(q_bias, "shard", axis=0, tiled=True),
        lax.all_gather(v_bias, "shard", axis=0, tiled=True),
        lax.all_gather(out_weight, "shard", axis=0, tiled=True),
        lax.all_gather(out_bias, "shard", axis=0, tiled=True),
    )
    first_norm_gain = attention_complete[0].astype(single_float)
    token_rows = images.reshape(-1, width).astype(single_float)
    first_standardized, first_scale_factor = norm_statistics(token_rows)
    first_normalized = (
        first_standardized * first_norm_gain + attention_complete[1].astype(single_float)
    ).astype(brain_float16)
    bias_all = jnp.concatenate(
        [
            attention_complete[3].astype(single_float),
            jnp.zeros((width,), single_float),
            attention_complete[4].astype(single_float),
        ]
    )
    qkv = (matmul(first_normalized, attention_complete[2]) + bias_all).astype(brain_float16)
    query = qkv[:, :width].reshape(count, seq, heads, head)
    keys = qkv[:, width : 2 * width].reshape(count, seq, heads, head)
    values = qkv[:, 2 * width :].reshape(count, seq, heads, head)
    scores = jnp.einsum("nqhe,nkhe->nhqk", query, keys, preferred_element_type=single_float) * scale
    top = jnp.max(scores, axis=-1, keepdims=True)
    total = jnp.sum(jnp.exp(scores - top), axis=-1, keepdims=True)
    lse = top + jnp.log(total)
    prob_b = jnp.exp(scores - lse).astype(brain_float16)
    context = (
        jnp.einsum("nhqk,nkhe->nqhe", prob_b, values, preferred_element_type=single_float)
        .astype(brain_float16)
        .reshape(-1, width)
    )
    hidden_activation = (
        token_rows
        + matmul(context, attention_complete[5])
        + attention_complete[6].astype(single_float)
    )
    perceptron_complete = (
        lax.all_gather(ln2_gain, "shard", axis=0, tiled=True),
        lax.all_gather(second_norm_bias, "shard", axis=0, tiled=True),
        lax.all_gather(up_weight, "shard", axis=0, tiled=True),
        lax.all_gather(up_bias, "shard", axis=0, tiled=True),
        lax.all_gather(down_weight, "shard", axis=0, tiled=True),
        lax.all_gather(down_bias, "shard", axis=0, tiled=True),
    )
    second_norm_gain = perceptron_complete[0].astype(single_float)
    second_standardized, second_scale_factor = norm_statistics(hidden_activation)
    second_normalized = (
        second_standardized * second_norm_gain + perceptron_complete[1].astype(single_float)
    ).astype(brain_float16)
    pre = matmul(second_normalized, perceptron_complete[2]) + perceptron_complete[3].astype(
        single_float
    )
    act, slope = gelu_parts(pre)
    act_b = act.astype(brain_float16)
    result = (
        hidden_activation
        + matmul(act_b, perceptron_complete[4])
        + perceptron_complete[5].astype(single_float)
    ).astype(brain_float16)
    perceptron_backward = (
        lax.all_gather(ln2_gain, "shard", axis=0, tiled=True),
        lax.all_gather(second_norm_bias, "shard", axis=0, tiled=True),
        lax.all_gather(up_weight, "shard", axis=0, tiled=True),
        lax.all_gather(up_bias, "shard", axis=0, tiled=True),
        lax.all_gather(down_weight, "shard", axis=0, tiled=True),
        lax.all_gather(down_bias, "shard", axis=0, tiled=True),
    )
    cot = cotangent.reshape(-1, width)
    cotangent_float32 = cot.astype(single_float)
    g_down_bias = jnp.sum(cotangent_float32, axis=0)
    g_down = matmul(act_b.T, cot)
    dpre = matmul(cot, perceptron_backward[4].T) * slope
    dpre_b = dpre.astype(brain_float16)
    g_up_bias = jnp.sum(dpre, axis=0)
    g_up = matmul(second_normalized.T, dpre_b)
    second_normalized_gradient = matmul(dpre_b, perceptron_backward[2].T)
    second_norm_gain_gradient = jnp.sum(second_normalized_gradient * second_standardized, axis=0)
    g_ln2_bias = jnp.sum(second_normalized_gradient, axis=0)
    middle_gradient = cotangent_float32 + norm_backward(
        second_normalized_gradient,
        second_standardized,
        second_scale_factor,
        perceptron_backward[0].astype(single_float),
    )
    mlp_grads = (second_norm_gain_gradient, g_ln2_bias, g_up, g_up_bias, g_down, g_down_bias)
    mlp_pieces = (
        lax.psum_scatter(
            mlp_grads[0].astype(jnp.bfloat16), "shard", scatter_dimension=0, tiled=True
        ).astype(jnp.float32),
        lax.psum_scatter(
            mlp_grads[1].astype(jnp.bfloat16), "shard", scatter_dimension=0, tiled=True
        ).astype(jnp.float32),
        lax.psum_scatter(
            mlp_grads[2].astype(jnp.bfloat16), "shard", scatter_dimension=0, tiled=True
        ).astype(jnp.float32),
        lax.psum_scatter(
            mlp_grads[3].astype(jnp.bfloat16), "shard", scatter_dimension=0, tiled=True
        ).astype(jnp.float32),
        lax.psum_scatter(
            mlp_grads[4].astype(jnp.bfloat16), "shard", scatter_dimension=0, tiled=True
        ).astype(jnp.float32),
        lax.psum_scatter(
            mlp_grads[5].astype(jnp.bfloat16), "shard", scatter_dimension=0, tiled=True
        ).astype(jnp.float32),
    )
    p_ln2_gain, p_ln2_bias, p_up, p_up_bias, p_down, p_down_bias = mlp_pieces
    attention_backward = (
        lax.all_gather(ln1_gain, "shard", axis=0, tiled=True),
        lax.all_gather(first_norm_bias, "shard", axis=0, tiled=True),
        lax.all_gather(qkv_weight, "shard", axis=0, tiled=True),
        lax.all_gather(q_bias, "shard", axis=0, tiled=True),
        lax.all_gather(v_bias, "shard", axis=0, tiled=True),
        lax.all_gather(out_weight, "shard", axis=0, tiled=True),
        lax.all_gather(out_bias, "shard", axis=0, tiled=True),
    )
    dmiddle_b = middle_gradient.astype(brain_float16)
    g_out_bias = jnp.sum(middle_gradient, axis=0)
    g_out = matmul(context.T, dmiddle_b)
    dcontext = (
        matmul(dmiddle_b, attention_backward[5].T)
        .astype(brain_float16)
        .reshape(count, seq, heads, head)
    )
    again = jnp.einsum("nqhe,nkhe->nhqk", query, keys, preferred_element_type=single_float) * scale
    prob = jnp.exp(again - lse)
    prob_again = prob.astype(brain_float16)
    dprob = jnp.einsum("nqhe,nkhe->nhqk", dcontext, values, preferred_element_type=single_float)
    dvalue = jnp.einsum(
        "nhqk,nqhe->nkhe", prob_again, dcontext, preferred_element_type=single_float
    ).reshape(-1, width)
    delta = jnp.sum(prob * dprob, axis=-1, keepdims=True)
    dscore = (prob * (dprob - delta) * scale).astype(brain_float16)
    dquery = jnp.einsum(
        "nhqk,nkhe->nqhe", dscore, keys, preferred_element_type=single_float
    ).reshape(-1, width)
    dkey = jnp.einsum(
        "nhqk,nqhe->nkhe", dscore, query, preferred_element_type=single_float
    ).reshape(-1, width)
    g_q_bias = jnp.sum(dquery, axis=0)
    g_v_bias = jnp.sum(dvalue, axis=0)
    dqkv = jnp.concatenate([dquery, dkey, dvalue], axis=1).astype(brain_float16)
    g_qkv = matmul(first_normalized.T, dqkv)
    first_normalized_gradient = matmul(dqkv, attention_backward[2].T)
    first_norm_gain_gradient = jnp.sum(first_normalized_gradient * first_standardized, axis=0)
    g_ln1_bias = jnp.sum(first_normalized_gradient, axis=0)
    input_gradient = (
        middle_gradient
        + norm_backward(
            first_normalized_gradient,
            first_standardized,
            first_scale_factor,
            attention_backward[0].astype(single_float),
        )
    ).astype(brain_float16)
    attn_grads = (
        first_norm_gain_gradient,
        g_ln1_bias,
        g_qkv,
        g_q_bias,
        g_v_bias,
        g_out,
        g_out_bias,
    )
    attn_pieces = (
        lax.psum_scatter(
            attn_grads[0].astype(jnp.bfloat16), "shard", scatter_dimension=0, tiled=True
        ).astype(jnp.float32),
        lax.psum_scatter(
            attn_grads[1].astype(jnp.bfloat16), "shard", scatter_dimension=0, tiled=True
        ).astype(jnp.float32),
        lax.psum_scatter(
            attn_grads[2].astype(jnp.bfloat16), "shard", scatter_dimension=0, tiled=True
        ).astype(jnp.float32),
        lax.psum_scatter(
            attn_grads[3].astype(jnp.bfloat16), "shard", scatter_dimension=0, tiled=True
        ).astype(jnp.float32),
        lax.psum_scatter(
            attn_grads[4].astype(jnp.bfloat16), "shard", scatter_dimension=0, tiled=True
        ).astype(jnp.float32),
        lax.psum_scatter(
            attn_grads[5].astype(jnp.bfloat16), "shard", scatter_dimension=0, tiled=True
        ).astype(jnp.float32),
        lax.psum_scatter(
            attn_grads[6].astype(jnp.bfloat16), "shard", scatter_dimension=0, tiled=True
        ).astype(jnp.float32),
    )
    p_ln1_gain, p_ln1_bias, p_qkv, p_q_bias, p_v_bias, p_out, p_out_bias = attn_pieces
    (
        p_ln1_gain,
        p_ln1_bias,
        p_qkv,
        p_q_bias,
        p_v_bias,
        p_out,
        p_out_bias,
        p_ln2_gain,
        p_ln2_bias,
        p_up,
        p_up_bias,
        p_down,
        p_down_bias,
    ) = lax.psum(
        (
            p_ln1_gain,
            p_ln1_bias,
            p_qkv,
            p_q_bias,
            p_v_bias,
            p_out,
            p_out_bias,
            p_ln2_gain,
            p_ln2_bias,
            p_up,
            p_up_bias,
            p_down,
            p_down_bias,
        ),
        "rep",
    )
    return (
        result.reshape(count, seq, width),
        input_gradient.reshape(count, seq, width),
        p_ln1_gain,
        p_ln1_bias,
        p_qkv,
        p_q_bias,
        p_v_bias,
        p_out,
        p_out_bias,
        p_ln2_gain,
        p_ln2_bias,
        p_up,
        p_up_bias,
        p_down,
        p_down_bias,
    )


def solution(mesh):
    in_specs = (
        P(("rep", "shard"), None, None),
        P("shard"),
        P("shard"),
        P("shard", None),
        P("shard"),
        P("shard"),
        P("shard", None),
        P("shard"),
        P("shard"),
        P("shard"),
        P("shard", None),
        P("shard"),
        P("shard", None),
        P("shard"),
        P(("rep", "shard"), None, None),
    )
    out_specs = (
        P(("rep", "shard"), None, None),
        P(("rep", "shard"), None, None),
        P("shard"),
        P("shard"),
        P("shard", None),
        P("shard"),
        P("shard"),
        P("shard", None),
        P("shard"),
        P("shard"),
        P("shard"),
        P("shard", None),
        P("shard"),
        P("shard", None),
        P("shard"),
    )
    return jax.shard_map(
        per_device, mesh=mesh, in_specs=in_specs, out_specs=out_specs, check_vma=False
    )
```

profile of v0, /device:TPU:1, one launch (start us, length us, event | category | flops | bytes accessed | tf_op | source)
XLA Modules:
  0.0 828.6 jit_solution(5341018697626411092)
XLA Ops:
  48.1 13.0 %all-gather.14.cloned.1.call-done = bf16[768,2304]{1,0:T(8,128)(2,1)} async-done(((bf16[384,2304]{1,0:T(8,128)(2,1)}), bf16[768,2304]{1,0:T(8,128)(2,1)}) %all-gather.14.cloned.1.call-update) | async-done | bytes 3538960 | tf_op jit(solution)/shard_map/all_gather | solution.py:62
  61.1 6.3 add_convert_fusion
  68.8 5.8 reshape.201
  74.6 6.0 copy.66
  85.0 6.0 copy.65
  126.3 23.3 %all-gather.18.cloned.1.call-done = bf16[768,3072]{1,0:T(8,128)(2,1)} async-done(((bf16[384,3072]{1,0:T(8,128)(2,1)}), bf16[768,3072]{1,0:T(8,128)(2,1)}) %all-gather.18.cloned.1.call-update) | async-done | bytes 4718608 | tf_op jit(solution)/shard_map/all_gather | solution.py:103
  149.7 13.6 %multiply_convert_fusion.1 = (bf16[985,3072]{1,0:T(8,128)(2,1)}, f32[985,3072]{1,0:T(8,128)}) fusion(f32[3072]{0:T(1024)S(1)} %bitcast.46, bf16[768,3072]{1,0:T(8,128)(2,1)} %all-gather.18.cloned.1.call-done, f32[985,768]{1,0:T(8,128)} %copy-done.5, f32[768]{0:T(1024)S(1)} %copy-done.25, f32[768]{0:T(1024)S(1)} %reshape.186, f32[985]{0:T(1024)S(1)} %add_rsqrt_fusion.1, ...), kind=kOutput, calls=%fused_computation.12 | convolution fusion | flops 4669751296 | bytes 25926344 | tf_op jit(solution)/shard_map/dot_general | solution.py:10
  163.3 50.4 %all-gather.20.cloned.1.call-done = bf16[3072,768]{1,0:T(8,128)(2,1)} async-done(((bf16[1536,768]{1,0:T(8,128)(2,1)}), bf16[3072,768]{1,0:T(8,128)(2,1)}) %all-gather.20.cloned.1.call-update) | async-done | bytes 4718608 | tf_op jit(solution)/shard_map/all_gather | solution.py:105
  213.7 11.6 %fusion.48 = (bf16[3072]{0:T(1024)(128)(2,1)S(1)}, bf16[985,3072]{1,0:T(8,128)(2,1)S(1)}) fusion(f32[985,3072]{1,0:T(8,128)} %get-tuple-element.55, f32[3072]{0:T(1024)S(1)} %bitcast.47, bf16[985,768]{1,0:T(8,128)(2,1)S(1)} %copy-done.15, bf16[3072,768]{1,0:T(8,128)(2,1)} %all-gather.20.cloned.1.call-done), kind=kOutput, calls=%fused_computation.97 | convolution fusion | flops 4684121088 | bytes 24405504 | tf_op jit(solution)/shard_map/dot_general | solution.py:10
  244.3 6.2 copy.71
  250.5 9.5 %bitcast_convert_fusion = (bf16[5,197,12,64]{1,3,2,0:T(8,128)(2,1)S(1)}, f32[5,12,64,197]{3,2,1,0:T(8,128)}) fusion(bf16[5,197,12,64]{1,3,2,0:T(8,128)(2,1)} %copy.71, f32[5,12,197,197]{2,3,1,0:T(8,128)} %copy-done, f32[5,12,197]{2,1,0:T(8,128)S(1)} %copy-done.20), kind=kOutput, calls=%fused_computation.27 | convolution fusion | flops 305795232 | bytes 15413280 | tf_op jit(solution)/shard_map/nhqk,nqhe->nkhe/dot_general | solution.py:191
  260.0 6.2 fusion.49
  275.1 20.7 %bitcast_convert_fusion.1 = (bf16[5,197,12,64]{1,3,2,0:T(8,128)(2,1)}, f32[5,12,64,197]{3,2,1,0:T(8,128)}) fusion(bf16[5,197,12,64]{1,3,2,0:T(8,128)(2,1)S(1)} %copy-done.4, f32[5,12,197,197]{2,3,1,0:T(8,128)} %fusion.49, f32[5,12,197,197]{2,3,1,0:T(8,128)} %copy-done, f32[5,12,197]{2,1,0:T(8,128)S(1)} %copy-done.20), kind=kOutput, calls=%fused_computation.29 | convolution fusion | flops 319778464 | bytes 24727440 | tf_op jit(solution)/shard_map/nhqk,nkhe->nqhe/dot_general | solution.py:196
  300.4 6.1 reshape.158
  306.6 19.3 %convert_bitcast_fusion = bf16[5,197,12,64]{1,3,2,0:T(8,128)(2,1)} fusion(bf16[5,197,12,64]{1,3,2,0:T(8,128)(2,1)S(1)} %copy-done.3, f32[5,12,197,197]{2,3,1,0:T(8,128)} %fusion.49, f32[5,12,197,197]{2,3,1,0:T(8,128)} %copy-done, f32[5,12,197]{2,1,0:T(8,128)S(1)} %copy-done.20), kind=kOutput, calls=%fused_computation.49 | convolution fusion | flops 319778464 | bytes 21701520 | tf_op jit(solution)/shard_map/nhqk,nqhe->nkhe/dot_general | solution.py:199
  337.0 6.1 convolution_convert_fusion.2
  344.5 9.7 %convolution_convert_fusion = bf16[3072,768]{1,0:T(8,128)(2,1)} fusion(bf16[985,3072]{1,0:T(8,128)(2,1)} %get-tuple-element.54, bf16[985,768]{1,0:T(8,128)(2,1)S(1)} %copy-done.16), kind=kOutput, calls=%fused_computation.23 | convolution fusion | flops 4650172416 | bytes 12283392 | tf_op jit(solution)/shard_map/dot_general | solution.py:10
  356.1 9.8 %convolution_convert_fusion.1 = bf16[768,3072]{1,0:T(8,128)(2,1)} fusion(bf16[985,3072]{1,0:T(8,128)(2,1)} %copy-done.37, f32[985,768]{1,0:T(8,128)S(1)} %copy-done.7, f32[768]{0:T(1024)S(1)} %copy-done.25, f32[768]{0:T(1024)S(1)} %reshape.186, f32[985]{0:T(1024)S(1)} %add_rsqrt_fusion.1, f32[985]{0:T(1024)S(1)} %broadcast_multiply_fusion.5), kind=kOutput, calls=%fused_computation.24 | convolution fusion | flops 4653955072 | bytes 13810376 | tf_op jit(solution)/shard_map/dot_general | solution.py:10
  374.0 10.1 %add_convert_fusion.2 = bf16[985,768]{1,0:T(8,128)(2,1)} fusion(f32[985,768]{1,0:T(8,128)S(1)} %copy-done.7, bf16[985,3072]{1,0:T(8,128)(2,1)} %get-tuple-element.54, bf16[3072,768]{1,0:T(8,128)(2,1)} %all-gather.20.cloned.1.call-done, f32[768]{0:T(1024)S(1)} %reshape.189), kind=kOutput, calls=%fused_computation.40 | convolution fusion | flops 4650083328 | bytes 15312384 | tf_op jit(solution)/shard_map/dot_general | solution.py:10
  392.3 8.6 %multiply_reduce_fusion.4 = (bf16[768]{0:T(1024)(128)(2,1)S(1)}, f32[985]{0:T(1024)S(1)}, f32[985]{0:T(1024)S(1)}, bf16[768]{0:T(1024)(128)(2,1)S(1)}, f32[985,768]{1,0:T(8,128)S(1)}) fusion(f32[985,768]{1,0:T(8,128)S(1)} %copy-done.12, f32[985]{0:T(1024)S(1)} %rsqrt.20, f32[985]{0:T(1024)S(1)} %div.27, f32[768]{0:T(1024)S(1)} %reshape.181, ...), kind=kOutput, calls=%fused_computation.32 | convolution fusion | flops 3492664576 | bytes 14151568 | tf_op jit(solution)/shard_map/dot_general | solution.py:10
  406.0 6.9 all-reduce.10
  413.6 40.4 %reduce-scatter.11.cloned.1.call-done = bf16[1536,768]{1,0:T(8,128)(2,1)} async-done(((bf16[3072,768]{1,0:T(8,128)(2,1)}), bf16[1536,768]{1,0:T(8,128)(2,1)}) %reduce-scatter.11.cloned.1.call-update) | async-done | bytes 2359312 | tf_op jit(solution)/shard_map/reduce_scatter | solution.py:162
  453.9 63.0 %reduce-scatter.9.cloned.1.call-done = bf16[384,3072]{1,0:T(8,128)(2,1)} async-done(((bf16[768,3072]{1,0:T(8,128)(2,1)}), bf16[384,3072]{1,0:T(8,128)(2,1)}) %reduce-scatter.9.cloned.1.call-update) | async-done | bytes 2359312 | tf_op jit(solution)/shard_map/reduce_scatter | solution.py:156
  516.9 304.7 %all-reduce.12 = (f32[384]{0:T(512)}, f32[384]{0:T(512)}, f32[384,2304]{1,0:T(8,128)}, f32[384]{0:T(512)}, f32[384]{0:T(512)}, /*index=5*/f32[384,768]{1,0:T(8,1...) all-reduce(f32[384]{0:T(512)S(1)} %dynamic-slice_convert_fusion.8, ...), channel_id=1, replica_groups=mesh['rep'=16,'shard'=2] {'rep'}, use_global_device_ids=true, to_apply=%region_13.0 | all-reduce | flops 3543552 | bytes 21270528 | tf_op jit(solution)/shard_map/psum | solution.py:265
  (188 shorter events, 149.0 us)
Async XLA Ops:
  7.2 53.9 %all-gather.14.cloned.1.call-start = ((), (), s32[]{:S(2)}) async-start(), calls=%async_computation.4 | async-start | bytes 5308416 | tf_op jit(solution)/shard_map/all_gather | solution.py:62
  7.9 111.8 %all-gather.16.cloned.1.call-start = ((), (), s32[]{:S(2)}) async-start(), calls=%async_computation.5 | async-start | bytes 1769472 | tf_op jit(solution)/shard_map/all_gather | solution.py:65
  8.7 141.0 %all-gather.18.cloned.1.call-start = ((), (), s32[]{:S(2)}) async-start(), calls=%async_computation.6 | async-start | bytes 7077888 | tf_op jit(solution)/shard_map/all_gather | solution.py:103
  9.4 204.3 %all-gather.20.cloned.1.call-start = ((), (), s32[]{:S(2)}) async-start(), calls=%async_computation.7 | async-start | bytes 7077888 | tf_op jit(solution)/shard_map/all_gather | solution.py:105
  10.0 403.6 %reduce-scatter.7.cloned.1.call-start = ((), (), s32[]{:S(2)}) async-start(), calls=%async_computation.9 | async-start | bytes 1769472 | tf_op jit(solution)/shard_map/reduce_scatter | solution.py:243
  10.4 6.7 copy-start.28
  10.4 9.9 %copy-start.29 = (bf16[384]{0:T(512)(128)(2,1)S(1)}, bf16[384]{0:T(512)(128)(2,1)}, u32[]{:S(2)}) copy-start(bf16[384]{0:T(512)(128)(2,1)} %param.19) | copy-start | bytes 2308
  10.4 13.5 %copy-start.30 = (bf16[384]{0:T(512)(128)(2,1)S(1)}, bf16[384]{0:T(512)(128)(2,1)}, u32[]{:S(2)}) copy-start(bf16[384]{0:T(512)(128)(2,1)} %param.20) | copy-start | bytes 2308
  10.5 17.4 %copy-start.31 = (bf16[384]{0:T(512)(128)(2,1)S(1)}, bf16[384]{0:T(512)(128)(2,1)}, u32[]{:S(2)}) copy-start(bf16[384]{0:T(512)(128)(2,1)} %param.22) | copy-start | bytes 2308
  10.5 21.7 %copy-start.32 = (bf16[384]{0:T(512)(128)(2,1)S(1)}, bf16[384]{0:T(512)(128)(2,1)}, u32[]{:S(2)}) copy-start(bf16[384]{0:T(512)(128)(2,1)} %param.23) | copy-start | bytes 2308
  10.5 25.4 %copy-start.33 = (bf16[384]{0:T(512)(128)(2,1)S(1)}, bf16[384]{0:T(512)(128)(2,1)}, u32[]{:S(2)}) copy-start(bf16[384]{0:T(512)(128)(2,1)} %param.24) | copy-start | bytes 2308
  10.5 29.7 %copy-start.26 = (bf16[1536]{0:T(1024)(128)(2,1)S(1)}, bf16[1536]{0:T(1024)(128)(2,1)}, u32[]{:S(2)}) copy-start(bf16[1536]{0:T(1024)(128)(2,1)} %param.26) | copy-start | bytes 9220
  13.1 48.0 %copy-start.10 = (f32[985,768]{1,0:T(8,128)S(1)}, f32[985,768]{1,0:T(8,128)}, u32[]{:S(2)}) copy-start(f32[985,768]{1,0:T(8,128)} %reshape.162) | copy-start | bytes 9077764
  20.3 47.1 %copy-start.23 = (f32[768]{0:T(1024)}, f32[768]{0:T(1024)S(1)}, u32[]{:S(2)}) copy-start(f32[768]{0:T(1024)S(1)} %reshape.182) | copy-start | bytes 9220
  124.2 25.5 %copy-start.22 = (f32[2,1,1536]{2,1,0:T(1,128)S(1)}, f32[2,1,1536]{2,1,0:T(1,128)}, u32[]{:S(2)}) copy-start(f32[2,1,1536]{2,1,0:T(1,128)} %convert_element_type.226) | copy-start | bytes 36868
  124.2 25.5 %copy-start.25 = (f32[768]{0:T(1024)S(1)}, f32[768]{0:T(1024)}, u32[]{:S(2)}) copy-start(f32[768]{0:T(1024)} %reshape.187) | copy-start | bytes 9220
  149.7 64.1 %copy-start.15 = (bf16[985,768]{1,0:T(8,128)(2,1)S(1)}, bf16[985,768]{1,0:T(8,128)(2,1)}, u32[]{:S(2)}) copy-start(bf16[985,768]{1,0:T(8,128)(2,1)} %reshape.156) | copy-start | bytes 4538884
  213.7 11.6 %copy-start.6 = (f32[985,768]{1,0:T(8,128)S(1)}, f32[985,768]{1,0:T(8,128)}, u32[]{:S(2)}) copy-start(f32[985,768]{1,0:T(8,128)} %copy-done.5) | copy-start | bytes 9077764
  213.7 11.6 %copy-start.35 = (bf16[768,3072]{1,0:T(8,128)(2,1)S(1)}, bf16[768,3072]{1,0:T(8,128)(2,1)}, u32[]{:S(2)}) copy-start(bf16[768,3072]{1,0:T(8,128)(2,1)} %all-gather.18.cloned.1.call-done) | copy-start | bytes 14155780
  236.3 177.3 %reduce-scatter.5.cloned.1.call-start = ((), (), s32[]{:S(2)}) async-start(), calls=%async_computation.8 | async-start | bytes 5308416 | tf_op jit(solution)/shard_map/reduce_scatter | solution.py:234
  250.5 9.5 %copy-start.1 = (bf16[5,197,12,64]{1,3,2,0:T(8,128)(2,1)S(1)}, bf16[5,197,12,64]{1,3,2,0:T(8,128)(2,1)}, u32[]{:S(2)}) copy-start(bf16[5,197,12,64]{1,3,2,0:T(8,128)(2,1)} %copy.71) | copy-start | bytes 4538884
  343.1 110.8 %reduce-scatter.11.cloned.1.call-start = ((), (), s32[]{:S(2)}) async-start(), calls=%async_computation.11 | async-start | bytes 7077888 | tf_op jit(solution)/shard_map/reduce_scatter | solution.py:162
  354.2 162.7 %reduce-scatter.9.cloned.1.call-start = ((), (), s32[]{:S(2)}) async-start(), calls=%async_computation.10 | async-start | bytes 7077888 | tf_op jit(solution)/shard_map/reduce_scatter | solution.py:156
  392.3 8.7 %copy-start.9 = (f32[985,768]{1,0:T(8,128)S(1)}, f32[985,768]{1,0:T(8,128)}, u32[]{:S(2)}) copy-start(f32[985,768]{1,0:T(8,128)} %copy-done.8) | copy-start | bytes 9077764
  (22 other events, 69.7 us)
Sparse Core Ops, SparseCore 0:
  9.5 51.5 all-gather.13
  62.6 22.7 all-gather.15
  87.0 62.6 all-gather.17
  151.1 62.6 all-gather.19
  236.4 21.8 reduce-scatter.6
  343.2 47.7 reduce-scatter.4
  393.3 60.5 reduce-scatter.10
  456.8 60.0 reduce-scatter.8
where the time goes:
time: 832 us; the launch traced here: 829 us
  blocking collectives  345 us (41%)
  waiting for transfers between devices  193 us (23%)
  matrix products  154 us (19%)
  local copies, waits for them, and re-layouts  104 us (12%)
  between operations  16.2 us (2%)
  other arithmetic  16 us (2%)
    psum x1, blocking collectives, per_device(): lax.psum((p_ln1_gain, p_ln1_bias, p_qkv, p_q_bias, p_v_bias, p_out, p_out...  305 us
    dot_general x12, matrix products, matmul(): return jnp.dot(left, right, preferred_element_type=jnp.float32)  91.7 us
    reduce_scatter x1, waiting for transfers between devices, per_device(): lax.psum_scatter(mlp_grads[2].astype(jnp.bfloat16), 'shard', scatter_dime...  63 us
    all_gather x1, waiting for transfers between devices, per_device(): lax.all_gather(down_weight, 'shard', axis=0, tiled=True)  50.4 us
    reduce_scatter x1, waiting for transfers between devices, per_device(): lax.psum_scatter(mlp_grads[4].astype(jnp.bfloat16), 'shard', scatter_dime...  40.4 us
    all_gather x1, waiting for transfers between devices, per_device(): lax.all_gather(up_weight, 'shard', axis=0, tiled=True)  23.3 us
    dot_general x1, matrix products, per_device(): jnp.einsum('nhqk,nkhe->nqhe', dscore, keys, preferred_element_type=single...  20.7 us
    dot_general x1, matrix products, per_device(): jnp.einsum('nhqk,nqhe->nkhe', dscore, query, preferred_element_type=singl...  19.3 us
  transfers between devices with their start and end apart: 8, of which 5 were waited for; matrix products, arithmetic and copies ran while one was open for 29% of the time, Pallas kernels for 0%

commit v1 on v0

--- a/solution.py
+++ b/solution.py
@@ -31,6 +31,64 @@
     cdf = 0.5 * (1.0 + lax.erf(pre * 0.7071067811865476))
     dens = jnp.exp(-0.5 * pre * pre) * 0.3989422804014327
     return (pre * cdf, cdf + pre * dens)
+
+
+def swap(array, axis, size, step):
+    return lax.ppermute(array, axis, [(i, i ^ step) for i in range(size)])
+
+
+def pick(array, index, axis=0):
+    return lax.dynamic_index_in_dim(array, index, axis, keepdims=False)
+
+
+def join(mine, theirs, bit):
+    low = jnp.where(bit == 0, mine, theirs)
+    high = jnp.where(bit == 0, theirs, mine)
+    return jnp.concatenate([low, high], axis=0)
+
+
+def gather_rows(part, rep, core, side):
+    halves = part.reshape((2, part.shape[0] // 2) + part.shape[1:])
+    direct = swap(pick(halves, core), "shard", 2, 1)
+    other = join(direct, swap(direct, "rep", rep, 1), core)
+    return join(part, other, side)
+
+
+def add(kept, received):
+    return (kept.astype(jnp.float32) + received.astype(jnp.float32)).astype(jnp.bfloat16)
+
+
+def reduce_rows(whole, rep, place, side, scatter=True):
+    rows = whole.shape[0]
+    core = place & 1
+    parts = whole.astype(jnp.bfloat16).reshape((2, 2, rows // 4) + whole.shape[1:])
+    now = add(pick(parts, core, 1), swap(pick(parts, 1 - core, 1), "rep", rep, 1))
+    now = add(pick(now, side), swap(pick(now, 1 - side), "shard", 2, 1))
+    steps = []
+    step = 2
+    while step < rep:
+        bit = (place // step) & 1
+        if now.shape[0] % 16 == 0:
+            parts = now.reshape((2, now.shape[0] // 2) + now.shape[1:])
+            now = add(pick(parts, bit), swap(pick(parts, 1 - bit), "rep", rep, step))
+            steps.append(step)
+        else:
+            now = add(now, swap(now, "rep", rep, step))
+        step *= 2
+    for step in reversed([1] + steps):
+        bit = (place // step) & 1
+        now = join(now, swap(now, "rep", rep, step), bit)
+    return now.astype(jnp.float32)
+
+
+def reduce_small(whole, rep, place, side):
+    now = whole
+    step = 1
+    while step < rep:
+        now = now + swap(now, "rep", rep, step)
+        step *= 2
+    now = now.reshape((2, now.shape[0] // 2) + now.shape[1:])
+    return pick(now, side) + swap(pick(now, 1 - side), "shard", 2, 1)
 
 
 def per_device(
@@ -56,15 +114,40 @@
     scale = head ** (-0.5)
     single_float = jnp.float32
     brain_float16 = jnp.bfloat16
-    attention_complete = (
-        lax.all_gather(ln1_gain, "shard", axis=0, tiled=True),
-        lax.all_gather(first_norm_bias, "shard", axis=0, tiled=True),
-        lax.all_gather(qkv_weight, "shard", axis=0, tiled=True),
-        lax.all_gather(q_bias, "shard", axis=0, tiled=True),
-        lax.all_gather(v_bias, "shard", axis=0, tiled=True),
-        lax.all_gather(out_weight, "shard", axis=0, tiled=True),
-        lax.all_gather(out_bias, "shard", axis=0, tiled=True),
-    )
+    rep = lax.axis_size("rep")
+    place = lax.axis_index("rep")
+    side = lax.axis_index("shard")
+    core = place & 1
+    small = (
+        ln1_gain,
+        first_norm_bias,
+        q_bias,
+        v_bias,
+        out_bias,
+        ln2_gain,
+        second_norm_bias,
+        up_bias,
+        down_bias,
+    )
+    packed = jnp.concatenate(small)
+    theirs = swap(packed, "shard", 2, 1)
+    low = jnp.where(side == 0, packed, theirs)
+    high = jnp.where(side == 0, theirs, packed)
+    full = []
+    at = 0
+    for vector in small:
+        size = vector.shape[0]
+        full.append(jnp.concatenate([low[at : at + size], high[at : at + size]]))
+        at += size
+    qkv_full = gather_rows(qkv_weight, rep, core, side)
+    out_part, _ = lax.optimization_barrier((out_weight, qkv_full[:8, :128]))
+    out_full = gather_rows(out_part, rep, core, side)
+    up_part, _ = lax.optimization_barrier((up_weight, out_full[:8, :128]))
+    up_full = gather_rows(up_part, rep, core, side)
+    down_part, _ = lax.optimization_barrier((down_weight, up_full[:8, :128]))
+    down_full = gather_rows(down_part, rep, core, side)
+    attention_complete = (full[0], full[1], qkv_full, full[2], full[3], out_full, full[4])
+    attention_backward = attention_complete
     first_norm_gain = attention_complete[0].astype(single_float)
     token_rows = images.reshape(-1, width).astype(single_float)
     first_standardized, first_scale_factor = norm_statistics(token_rows)
@@ -97,14 +180,8 @@
         + matmul(context, attention_complete[5])
         + attention_complete[6].astype(single_float)
     )
-    perceptron_complete = (
-        lax.all_gather(ln2_gain, "shard", axis=0, tiled=True),
-        lax.all_gather(second_norm_bias, "shard", axis=0, tiled=True),
-        lax.all_gather(up_weight, "shard", axis=0, tiled=True),
-        lax.all_gather(up_bias, "shard", axis=0, tiled=True),
-        lax.all_gather(down_weight, "shard", axis=0, tiled=True),
-        lax.all_gather(down_bias, "shard", axis=0, tiled=True),
-    )
+    perceptron_complete = (full[5], full[6], up_full, full[7], down_full, full[8])
+    perceptron_backward = perceptron_complete
     second_norm_gain = perceptron_complete[0].astype(single_float)
     second_standardized, second_scale_factor = norm_statistics(hidden_activation)
     second_normalized = (
@@ -120,14 +197,6 @@
         + matmul(act_b, perceptron_complete[4])
         + perceptron_complete[5].astype(single_float)
     ).astype(brain_float16)
-    perceptron_backward = (
-        lax.all_gather(ln2_gain, "shard", axis=0, tiled=True),
-        lax.all_gather(second_norm_bias, "shard", axis=0, tiled=True),
-        lax.all_gather(up_weight, "shard", axis=0, tiled=True),
-        lax.all_gather(up_bias, "shard", axis=0, tiled=True),
-        lax.all_gather(down_weight, "shard", axis=0, tiled=True),
-        lax.all_gather(down_bias, "shard", axis=0, tiled=True),
-    )
     cot = cotangent.reshape(-1, width)
     cotangent_float32 = cot.astype(single_float)
     g_down_bias = jnp.sum(cotangent_float32, axis=0)
@@ -146,36 +215,8 @@
         perceptron_backward[0].astype(single_float),
     )
     mlp_grads = (second_norm_gain_gradient, g_ln2_bias, g_up, g_up_bias, g_down, g_down_bias)
-    mlp_pieces = (
-        lax.psum_scatter(
-            mlp_grads[0].astype(jnp.bfloat16), "shard", scatter_dimension=0, tiled=True
-        ).astype(jnp.float32),
-        lax.psum_scatter(
-            mlp_grads[1].astype(jnp.bfloat16), "shard", scatter_dimension=0, tiled=True
-        ).astype(jnp.float32),
-        lax.psum_scatter(
-            mlp_grads[2].astype(jnp.bfloat16), "shard", scatter_dimension=0, tiled=True
-        ).astype(jnp.float32),
-        lax.psum_scatter(
-            mlp_grads[3].astype(jnp.bfloat16), "shard", scatter_dimension=0, tiled=True
-        ).astype(jnp.float32),
-        lax.psum_scatter(
-            mlp_grads[4].astype(jnp.bfloat16), "shard", scatter_dimension=0, tiled=True
-        ).astype(jnp.float32),
-        lax.psum_scatter(
-            mlp_grads[5].astype(jnp.bfloat16), "shard", scatter_dimension=0, tiled=True
-        ).astype(jnp.float32),
-    )
-    p_ln2_gain, p_ln2_bias, p_up, p_up_bias, p_down, p_down_bias = mlp_pieces
-    attention_backward = (
-        lax.all_gather(ln1_gain, "shard", axis=0, tiled=True),
-        lax.all_gather(first_norm_bias, "shard", axis=0, tiled=True),
-        lax.all_gather(qkv_weight, "shard", axis=0, tiled=True),
-        lax.all_gather(q_bias, "shard", axis=0, tiled=True),
-        lax.all_gather(v_bias, "shard", axis=0, tiled=True),
-        lax.all_gather(out_weight, "shard", axis=0, tiled=True),
-        lax.all_gather(out_bias, "shard", axis=0, tiled=True),
-    )
+    p_down = reduce_rows(g_down, rep, place, side)
+    p_up = reduce_rows(g_up, rep, place, side)
     dmiddle_b = middle_gradient.astype(brain_float16)
     g_out_bias = jnp.sum(middle_gradient, axis=0)
     g_out = matmul(context.T, dmiddle_b)
@@ -224,62 +265,28 @@
         g_out,
         g_out_bias,
     )
-    attn_pieces = (
-        lax.psum_scatter(
-            attn_grads[0].astype(jnp.bfloat16), "shard", scatter_dimension=0, tiled=True
-        ).astype(jnp.float32),
-        lax.psum_scatter(
-            attn_grads[1].astype(jnp.bfloat16), "shard", scatter_dimension=0, tiled=True
-        ).astype(jnp.float32),
-        lax.psum_scatter(
-            attn_grads[2].astype(jnp.bfloat16), "shard", scatter_dimension=0, tiled=True
-        ).astype(jnp.float32),
-        lax.psum_scatter(
-            attn_grads[3].astype(jnp.bfloat16), "shard", scatter_dimension=0, tiled=True
-        ).astype(jnp.float32),
-        lax.psum_scatter(
-            attn_grads[4].astype(jnp.bfloat16), "shard", scatter_dimension=0, tiled=True
-        ).astype(jnp.float32),
-        lax.psum_scatter(
-            attn_grads[5].astype(jnp.bfloat16), "shard", scatter_dimension=0, tiled=True
-        ).astype(jnp.float32),
-        lax.psum_scatter(
-            attn_grads[6].astype(jnp.bfloat16), "shard", scatter_dimension=0, tiled=True
-        ).astype(jnp.float32),
-    )
-    p_ln1_gain, p_ln1_bias, p_qkv, p_q_bias, p_v_bias, p_out, p_out_bias = attn_pieces
-    (
-        p_ln1_gain,
-        p_ln1_bias,
-        p_qkv,
-        p_q_bias,
-        p_v_bias,
-        p_out,
-        p_out_bias,
-        p_ln2_gain,
-        p_ln2_bias,
-        p_up,
-        p_up_bias,
-        p_down,
-        p_down_bias,
-    ) = lax.psum(
-        (
-            p_ln1_gain,
-            p_ln1_bias,
-            p_qkv,
-            p_q_bias,
-            p_v_bias,
-            p_out,
-            p_out_bias,
-            p_ln2_gain,
-            p_ln2_bias,
-            p_up,
-            p_up_bias,
-            p_down,
-            p_down_bias,
-        ),
-        "rep",
-    )
+    p_out = reduce_rows(g_out, rep, place, side)
+    p_qkv = reduce_rows(g_qkv, rep, place, side)
+    vectors = (
+        first_norm_gain_gradient,
+        g_ln1_bias,
+        g_q_bias,
+        g_v_bias,
+        g_out_bias,
+        second_norm_gain_gradient,
+        g_ln2_bias,
+        g_up_bias,
+        g_down_bias,
+    )
+    packed = jnp.concatenate([v.reshape(2, -1) for v in vectors], axis=1)
+    summed = reduce_small(packed, rep, place, side).reshape(-1)
+    pieces = []
+    at = 0
+    for v in vectors:
+        size = v.shape[0] // 2
+        pieces.append(summed[at : at + size])
+        at += size
+    p_ln1_gain, p_ln1_bias, p_q_bias, p_v_bias, p_out_bias, p_ln2_gain, p_ln2_bias, p_up_bias, p_down_bias = pieces
     return (
         result.reshape(count, seq, width),
         input_gradient.reshape(count, seq, width),

time: 832 us -> 584 us (0.70)
  blocking collectives: 345 us -> 0 us
  starting transfers between devices: 0.32 us -> 57.2 us
  other arithmetic: 16 us -> 51 us
  local copies, waits for them, and re-layouts: 104 us -> 120 us
  between operations: 16.2 us -> 2.17 us
    psum x1 -> x0, blocking collectives: 305 us -> none  [per_device(): lax.psum((p_ln1_gain, p_ln1_bias, p_qkv, p_q_bias, p_v_bias, p_out, p_out...]
    ppermute x0 -> x50, waiting for transfers between devices: none -> 188 us  [swap(): return lax.ppermute(array, axis, [(i, i ^ step) for i in range(size)])]
    reduce_scatter x4 -> x0, waiting for transfers between devices: 103 us -> none  [the longest x1 63 us: per_device(): lax.psum_scatter(mlp_grads[2].astype(jnp.bfloat16), 'shard', scatter_dime...]
    all_gather x4 -> x0, waiting for transfers between devices: 86.8 us -> none  [the longest x1 50.4 us: per_device(): lax.all_gather(down_weight, 'shard', axis=0, tiled=True)]
    ppermute x0 -> x50, starting transfers between devices: none -> 57.2 us  [swap(): return lax.ppermute(array, axis, [(i, i ^ step) for i in range(size)])]
    all_gather x9 -> x0, blocking collectives: 33.6 us -> none  [the longest x1 4.27 us: per_device(): lax.all_gather(up_bias, 'shard', axis=0, tiled=True)]
    convert_element_type x9 -> x24, other arithmetic: 0.67 us -> 18.2 us  [the longest x20 9.82 us: add(): (kept.astype(jnp.float32) + received.astype(jnp.float32)).astype(jnp.bflo...]
    squeeze x0 -> x25, local copies, waits for them, and re-layouts: none -> 17.5 us  [pick(): return lax.dynamic_index_in_dim(array, index, axis, keepdims=False)]
  transfers between devices with their start and end apart: 8 -> 50, of which waited for: 5 -> 23; matrix products, arithmetic and copies ran while one was open for 29% -> 29% of each run, Pallas kernels for 0% -> 0%
where the time goes in v1:
time: 584 us; the launch traced here: 575 us
  waiting for transfers between devices  188 us (32%)
  matrix products  157 us (27%)
  local copies, waits for them, and re-layouts  120 us (21%)
  starting transfers between devices  57.2 us (10%)
  other arithmetic  51 us (9%)
    ppermute x50, waiting for transfers between devices, swap(): return lax.ppermute(array, axis, [(i, i ^ step) for i in range(size)])  188 us
    dot_general x12, matrix products, matmul(): return jnp.dot(left, right, preferred_element_type=jnp.float32)  88.8 us
    ppermute x50, starting transfers between devices, swap(): return lax.ppermute(array, axis, [(i, i ^ step) for i in range(size)])  57.2 us
    dot_general x1, matrix products, per_device(): jnp.einsum('nhqk,nkhe->nqhe', dscore, keys, preferred_element_type=single...  23.2 us
    dot_general x1, matrix products, per_device(): jnp.einsum('nhqk,nqhe->nkhe', dscore, query, preferred_element_type=singl...  22.2 us
    squeeze x25, local copies, waits for them, and re-layouts, pick(): return lax.dynamic_index_in_dim(array, index, axis, keepdims=False)  17.5 us
    unnamed x122, local copies, waits for them, and re-layouts  16.1 us
    select_n x24, other arithmetic, join(): low = jnp.where(bit == 0, mine, theirs)  14 us
  transfers between devices with their start and end apart: 50, of which 23 were waited for; matrix products, arithmetic and copies ran while one was open for 29% of the time, Pallas kernels for 0%

profile of v1, /device:TPU:1, one launch (start us, length us, event | category | flops | bytes accessed | tf_op | source)
XLA Modules:
  0.0 575.0 jit_solution(16941610970458875133)
XLA Ops:
  27.8 10.5 %collective-permute-done.1 = bf16[192,2304]{1,0:T(8,128)(2,1)} collective-permute-done((bf16[192,2304]{1,0:T(8,128)(2,1)}, bf16[192,2304]{1,0:T(8,128)(2,1)}, u32[]{:S(2)}, u32[]{:S(2)}) %collective-permute-start.1) | collective-permute-done | bytes 884768 | tf_op jit(solution)/shard_map/ppermute | solution.py:37
  46.5 17.1 %collective-permute-done.7 = bf16[768,768]{1,0:T(8,128)(2,1)} collective-permute-done((bf16[768,768]{1,0:T(8,128)(2,1)}, bf16[768,768]{1,0:T(8,128)(2,1)}, u32[]{:S(2)}, u32[]{:S(2)}) %collective-permute-start.7) | collective-permute-done | bytes 1179680 | tf_op jit(solution)/shard_map/ppermute | solution.py:37
  66.9 22.1 %collective-permute-done.5 = bf16[192,3072]{1,0:T(8,128)(2,1)} collective-permute-done((bf16[192,3072]{1,0:T(8,128)(2,1)}, bf16[192,3072]{1,0:T(8,128)(2,1)}, u32[]{:S(2)}, u32[]{:S(2)}) %collective-permute-start.5) | collective-permute-done | bytes 1179680 | tf_op jit(solution)/shard_map/ppermute | solution.py:37
  105.6 6.5 %copy.46 = bf16[5,197,12,64]{1,3,2,0:T(8,128)(2,1)} copy(bf16[5,197,12,64]{3,2,1,0:T(8,128)(2,1)} %reshape.454) | data formatting | bytes 3025920 | tf_op jit(solution)/shard_map/reshape | solution.py:166
  163.4 10.0 %multiply_convert_fusion.1 = (bf16[985,3072]{1,0:T(8,128)(2,1)}, f32[985,3072]{1,0:T(8,128)}) fusion(f32[3072]{0:T(1024)S(1)} %maximum_convert_fusion.4, bf16[384,3072]{1,0:T(8,128)(2,1)S(1)} %get-tuple-element.36, bf16[384,3072]{1,0:T(8,128)(2,1)S(1)} %get-tuple-element.35, f32[985,768]{1,0:T(8,128)S(1)} %get-tuple-element.105, f32[768]{0:T(1024)S(1)} %copy-done.47, ...), kind=kOutput, calls=%fused_computation.12 | convolution fusion | flops 4679188480 | bytes 25926344 | tf_op jit(solution)/shard_map/dot_general | solution.py:10
  173.5 15.4 %fusion.80 = (f32[3072]{0:T(1024)S(1)}, bf16[985,3072]{1,0:T(8,128)(2,1)S(1)}) fusion(f32[985,3072]{1,0:T(8,128)} %get-tuple-element.107, f32[3072]{0:T(1024)S(1)} %maximum_convert_fusion.4, bf16[985,768]{1,0:T(8,128)(2,1)S(1)} %copy-done.13, bf16[1536,768]{1,0:T(8,128)(2,1)S(1)} %get-tuple-element.34, bf16[1536,768]{1,0:T(8,128)(2,1)S(1)} %get-tuple-element.33), kind=kOutput, calls=%fused_computation.260 | convolution fusion | flops 4693558272 | bytes 24411648 | tf_op jit(solution)/shard_map/dot_general | solution.py:10
  194.5 7.8 %convolution_convert_fusion.1 = bf16[768,3072]{1,0:T(8,128)(2,1)} fusion(bf16[985,3072]{1,0:T(8,128)(2,1)S(1)} %get-tuple-element.115, f32[985,768]{1,0:T(8,128)S(1)} %get-tuple-element.105, f32[768]{0:T(1024)S(1)} %copy-done.47, f32[768]{0:T(1024)S(1)} %maximum_convert_fusion.10, f32[985]{0:T(1024)S(1)} %add_rsqrt_fusion.1, ...), kind=kOutput, calls=%fused_computation.24 | convolution fusion | flops 4653955072 | bytes 13810376 | tf_op jit(solution)/shard_map/dot_general | solution.py:10
  220.7 10.0 %bitcast_convert_fusion = (bf16[5,197,12,64]{1,3,2,0:T(8,128)(2,1)}, f32[5,12,64,197]{3,2,1,0:T(8,128)}) fusion(bf16[5,197,12,64]{1,3,2,0:T(8,128)(2,1)} %copy.51, f32[5,12,197,197]{2,3,1,0:T(8,128)} %copy-done, f32[5,12,197]{2,1,0:T(8,128)} %copy-done.31), kind=kOutput, calls=%fused_computation.33 | convolution fusion | flops 305795232 | bytes 15413280 | tf_op jit(solution)/shard_map/nhqk,nqhe->nkhe/dot_general | solution.py:232
  230.7 6.2 %fusion.81 = f32[5,12,197,197]{2,3,1,0:T(8,128)} fusion(bf16[5,197,12,64]{1,3,2,0:T(8,128)(2,1)S(1)} %copy-done.1, bf16[5,197,12,64]{1,3,2,0:T(8,128)(2,1)S(1)} %copy.47), kind=kOutput, calls=%fused_computation.261 | convolution fusion | flops 298053120 | bytes 12340080 | tf_op jit(solution)/shard_map/nqhe,nkhe->nhqk/dot_general | solution.py:231
  236.9 22.2 %convert_bitcast_fusion = bf16[5,197,12,64]{1,3,2,0:T(8,128)(2,1)} fusion(bf16[5,197,12,64]{1,3,2,0:T(8,128)(2,1)} %copy.45, f32[5,12,197,197]{2,3,1,0:T(8,128)} %fusion.81, f32[5,12,197,197]{2,3,1,0:T(8,128)} %copy-done, f32[5,12,197]{2,1,0:T(8,128)} %copy-done.31), kind=kOutput, calls=%fused_computation.76 | convolution fusion | flops 319778464 | bytes 21701520 | tf_op jit(solution)/shard_map/nhqk,nqhe->nkhe/dot_general | solution.py:240
  259.1 23.2 %bitcast_convert_fusion.1 = (bf16[5,197,12,64]{1,3,2,0:T(8,128)(2,1)}, f32[5,12,64,197]{3,2,1,0:T(8,128)}) fusion(bf16[5,197,12,64]{1,3,2,0:T(8,128)(2,1)S(1)} %copy-done.3, f32[5,12,197,197]{2,3,1,0:T(8,128)} %fusion.81, f32[5,12,197,197]{2,3,1,0:T(8,128)} %copy-done, f32[5,12,197]{2,1,0:T(8,128)} %copy-done.31), kind=kOutput, calls=%fused_computation.35 | convolution fusion | flops 319778464 | bytes 24727440 | tf_op jit(solution)/shard_map/nhqk,nkhe->nqhe/dot_general | solution.py:237
  282.3 10.0 %convolution_convert_fusion = bf16[3072,768]{1,0:T(8,128)(2,1)} fusion(bf16[985,3072]{1,0:T(8,128)(2,1)} %get-tuple-element.106, bf16[985,768]{1,0:T(8,128)(2,1)S(1)} %copy-done.13), kind=kOutput, calls=%fused_computation.23 | convolution fusion | flops 4650172416 | bytes 12283392 | tf_op jit(solution)/shard_map/dot_general | solution.py:10
  292.4 8.9 %add_convert_fusion.2 = bf16[985,768]{1,0:T(8,128)(2,1)} fusion(f32[985,768]{1,0:T(8,128)S(1)} %copy-done.7, f32[768]{0:T(1024)S(1)} %copy-done.46, bf16[985,3072]{1,0:T(8,128)(2,1)} %get-tuple-element.106, bf16[1536,768]{1,0:T(8,128)(2,1)S(1)} %copy-done.22, bf16[1536,768]{1,0:T(8,128)(2,1)S(1)} %copy-done.20), kind=kOutput, calls=%fused_computation.50 | convolution fusion | flops 4659520512 | bytes 15312384 | tf_op jit(solution)/shard_map/dot_general | solution.py:10
  331.4 9.2 %multiply_reduce_fusion.4 = (f32[768]{0:T(1024)S(1)}, f32[985]{0:T(1024)S(1)}, f32[985]{0:T(1024)S(1)}, f32[768]{0:T(1024)S(1)}, f32[985,768]{1,0:T(8,128)}) fusion(f32[985,768]{1,0:T(8,128)S(1)} %copy-done.9, f32[985]{0:T(1024)S(1)} %copy-done.40, f32[985]{0:T(1024)S(1)} %copy-done.38, f32[768]{0:T(1024)S(1)} %copy-done.42, ...), kind=kOutput, calls=%fused_computation.42 | convolution fusion | flops 3499742464 | bytes 14154640 | tf_op jit(solution)/shard_map/dot_general | solution.py:10
  341.3 8.4 %convolution_convert_fusion.2 = bf16[768,2304]{1,0:T(8,128)(2,1)} fusion(bf16[985,2304]{0,1:T(8,128)(2,1)} %copy-done.34, f32[985,768]{1,0:T(8,128)S(1)} %copy-done.9, f32[768]{0:T(1024)S(1)} %copy-done.45, f32[768]{0:T(1024)S(1)} %copy-done.42, f32[985]{0:T(1024)S(1)} %copy-done.40, f32[985]{0:T(1024)S(1)} %copy-done.38), kind=kOutput, calls=%fused_computation.25 | convolution fusion | flops 3491411712 | bytes 11117768 | tf_op jit(solution)/shard_map/dot_general | solution.py:10
  408.3 18.5 %collective-permute-done.15 = bf16[192,2304]{1,0:T(8,128)(2,1)S(1)} collective-permute-done((bf16[192,2304]{1,0:T(8,128)(2,1)S(1)}, bf16[192,2304]{1,0:T(8,128)(2,1)S(1)}, u32[]{:S(2)}, u32[]{:S(2)}) %collective-permute-start.15) | collective-permute-done | bytes 884768 | tf_op jit(solution)/shard_map/ppermute | solution.py:37
  430.0 8.0 %collective-permute-done.16 = bf16[96,2304]{1,0:T(8,128)(2,1)S(1)} collective-permute-done((bf16[96,2304]{1,0:T(8,128)(2,1)S(1)}, bf16[96,2304]{1,0:T(8,128)(2,1)S(1)}, u32[]{:S(2)}, u32[]{:S(2)}) %collective-permute-start.16) | collective-permute-done | bytes 442400 | tf_op jit(solution)/shard_map/ppermute | solution.py:37
  449.2 6.9 %collective-permute-done.42 = bf16[768,768]{1,0:T(8,128)(2,1)S(1)} collective-permute-done((bf16[768,768]{1,0:T(8,128)(2,1)S(1)}, bf16[768,768]{1,0:T(8,128)(2,1)S(1)}, u32[]{:S(2)}, u32[]{:S(2)}) %collective-permute-start.42) | collective-permute-done | bytes 1179680 | tf_op jit(solution)/shard_map/ppermute | solution.py:37
  458.1 23.4 %collective-permute-done.33 = bf16[192,3072]{1,0:T(8,128)(2,1)S(1)} collective-permute-done((bf16[192,3072]{1,0:T(8,128)(2,1)S(1)}, bf16[192,3072]{1,0:T(8,128)(2,1)S(1)}, u32[]{:S(2)}, u32[]{:S(2)}) %collective-permute-start.33) | collective-permute-done | bytes 1179680 | tf_op jit(solution)/shard_map/ppermute | solution.py:37
  484.1 10.7 %collective-permute-done.34 = bf16[96,3072]{1,0:T(8,128)(2,1)S(1)} collective-permute-done((bf16[96,3072]{1,0:T(8,128)(2,1)S(1)}, bf16[96,3072]{1,0:T(8,128)(2,1)S(1)}, u32[]{:S(2)}, u32[]{:S(2)}) %collective-permute-start.34) | collective-permute-done | bytes 589856 | tf_op jit(solution)/shard_map/ppermute | solution.py:37
  495.3 9.0 %collective-permute-done.21 = bf16[96,2304]{1,0:T(8,128)(2,1)S(1)} collective-permute-done((bf16[96,2304]{1,0:T(8,128)(2,1)S(1)}, bf16[96,2304]{1,0:T(8,128)(2,1)S(1)}, u32[]{:S(2)}, u32[]{:S(2)}) %collective-permute-start.21) | collective-permute-done | bytes 442400 | tf_op jit(solution)/shard_map/ppermute | solution.py:37
  507.2 10.0 %collective-permute-done.45 = bf16[96,768]{1,0:T(8,128)(2,1)S(1)} collective-permute-done((bf16[96,768]{1,0:T(8,128)(2,1)S(1)}, bf16[96,768]{1,0:T(8,128)(2,1)S(1)}, u32[]{:S(2)}, u32[]{:S(2)}) %collective-permute-start.45) | collective-permute-done | bytes 147488 | tf_op jit(solution)/shard_map/ppermute | solution.py:37
  520.4 6.5 %collective-permute-done.46 = bf16[96,768]{1,0:T(8,128)(2,1)S(1)} collective-permute-done((bf16[96,768]{1,0:T(8,128)(2,1)S(1)}, bf16[96,768]{1,0:T(8,128)(2,1)S(1)}, u32[]{:S(2)}, u32[]{:S(2)}) %collective-permute-start.46) | collective-permute-done | bytes 147488 | tf_op jit(solution)/shard_map/ppermute | solution.py:37
  549.8 6.9 %collective-permute-start.49 = (bf16[768,768]{1,0:T(8,128)(2,1)S(1)}, bf16[768,768]{1,0:T(8,128)(2,1)S(1)}, u32[]{:S(2)}, u32[]{:S(2)}) collective-permute-start(bf16[768,768]{1,0:T(8,128)(2,1)S(1)} %pad_maximum_fusion.16), channel_id=1, source_target_pairs={{0,2},{2,0},{4,6},{6,4},{8,10},{10,8},{12,14},{14,12},{16,18},{18,... | collective-permute-start | bytes 3538952 | tf_op jit(solution)/shard_map/ppermute | solution.py:37
  (379 shorter events, 285.6 us)
Async XLA Ops:
  8.4 17.5 %collective-permute-start = (bf16[4608]{0:T(1024)(128)(2,1)S(1)}, bf16[4608]{0:T(1024)(128)(2,1)S(1)}, u32[]{:S(2)}, u32[]{:S(2)}) collective-permute-start(bf16[4608]{0:T(1024)(128)(2,1)S(1)} %dynamic-update-slice.20), channel_id=1, source_target_pairs={{0,1},{1,0},{2,3},{3,2},{4,5},{5,4},{6,7},{7,6},{8,9},{9,8},{10,11... | collective-permute-start | bytes 27656 | tf_op jit(solution)/shard_map/ppermute | solution.py:37
  11.6 30.0 %collective-permute-start.3 = (bf16[192,768]{1,0:T(8,128)(2,1)S(1)}, bf16[192,768]{1,0:T(8,128)(2,1)}, u32[]{:S(2)}, u32[]{:S(2)}) collective-permute-start(bf16[192,768]{1,0:T(8,128)(2,1)S(1)} %dynamic-slice_bitcast_fusion.16), channel_id=1, source_target_pairs={{0,1},{1,0},{2,3},{3,2},{4,5},{5,4},{6,7},{7,6},{8,9},{9,8},{10,11... | collective-permute-start | bytes 884744 | tf_op jit(solution)/shard_map/ppermute | solution.py:37
  14.0 24.4 %collective-permute-start.1 = (bf16[192,2304]{1,0:T(8,128)(2,1)}, bf16[192,2304]{1,0:T(8,128)(2,1)}, u32[]{:S(2)}, u32[]{:S(2)}) collective-permute-start(bf16[192,2304]{1,0:T(8,128)(2,1)} %dynamic-slice_bitcast_fusion.8), channel_id=1, source_target_pairs={{0,1},{1,0},{2,3},{3,2},{4,5},{5,4},{6,7},{7,6},{8,9},{9,8},{10,11... | collective-permute-start | bytes 2654216 | tf_op jit(solution)/shard_map/ppermute | solution.py:37
  17.8 45.9 %collective-permute-start.7 = (bf16[768,768]{1,0:T(8,128)(2,1)}, bf16[768,768]{1,0:T(8,128)(2,1)}, u32[]{:S(2)}, u32[]{:S(2)}) collective-permute-start(bf16[768,768]{1,0:T(8,128)(2,1)} %dynamic-slice_bitcast_fusion.5), channel_id=1, source_target_pairs={{0,1},{1,0},{2,3},{3,2},{4,5},{5,4},{6,7},{7,6},{8,9},{9,8},{10,11... | collective-permute-start | bytes 3538952 | tf_op jit(solution)/shard_map/ppermute | solution.py:37
  18.9 70.0 %collective-permute-start.5 = (bf16[192,3072]{1,0:T(8,128)(2,1)}, bf16[192,3072]{1,0:T(8,128)(2,1)}, u32[]{:S(2)}, u32[]{:S(2)}) collective-permute-start(bf16[192,3072]{1,0:T(8,128)(2,1)} %dynamic-slice_bitcast_fusion.6), channel_id=1, source_target_pairs={{0,1},{1,0},{2,3},{3,2},{4,5},{5,4},{6,7},{7,6},{8,9},{9,8},{10,11... | collective-permute-start | bytes 3538952 | tf_op jit(solution)/shard_map/ppermute | solution.py:37
  38.4 52.4 %collective-permute-start.2 = (bf16[192,2304]{1,0:T(8,128)(2,1)}, bf16[192,2304]{1,0:T(8,128)(2,1)S(1)}, u32[]{:S(2)}, u32[]{:S(2)}) collective-permute-start(bf16[192,2304]{1,0:T(8,128)(2,1)} %collective-permute-done.1), channel_id=1, source_target_pairs={{0,2},{2,0},{4,6},{6,4},{8,10},{10,8},{12,14},{14,12},{16,18},{18,... | collective-permute-start | bytes 2654216 | tf_op jit(solution)/shard_map/ppermute | solution.py:37
  63.6 96.4 %collective-permute-start.8 = (bf16[768,768]{1,0:T(8,128)(2,1)}, bf16[768,768]{1,0:T(8,128)(2,1)}, u32[]{:S(2)}, u32[]{:S(2)}) collective-permute-start(bf16[768,768]{1,0:T(8,128)(2,1)} %collective-permute-done.7), channel_id=1, source_target_pairs={{0,2},{2,0},{4,6},{6,4},{8,10},{10,8},{12,14},{14,12},{16,18},{18,... | collective-permute-start | bytes 3538952 | tf_op jit(solution)/shard_map/ppermute | solution.py:37
  88.9 67.1 %collective-permute-start.6 = (bf16[192,3072]{1,0:T(8,128)(2,1)}, bf16[192,3072]{1,0:T(8,128)(2,1)}, u32[]{:S(2)}, u32[]{:S(2)}) collective-permute-start(bf16[192,3072]{1,0:T(8,128)(2,1)} %collective-permute-done.5), channel_id=1, source_target_pairs={{0,2},{2,0},{4,6},{6,4},{8,10},{10,8},{12,14},{14,12},{16,18},{18,... | collective-permute-start | bytes 3538952 | tf_op jit(solution)/shard_map/ppermute | solution.py:37
  302.2 47.5 %collective-permute-start.23 = (bf16[2,192,768]{2,1,0:T(8,128)(2,1)}, bf16[2,192,768]{2,1,0:T(8,128)(2,1)}, u32[]{:S(2)}, u32[]{:S(2)}) collective-permute-start(bf16[2,192,768]{2,1,0:T(8,128)(2,1)} %dynamic-slice_bitcast_fusion.11), channel_id=1, source_target_pairs={{0,2},{2,0},{4,6},{6,4},{8,10},{10,8},{12,14},{14,12},{16,18},{18,... | collective-permute-start | bytes 1769480 | tf_op jit(solution)/shard_map/ppermute | solution.py:37
  340.7 33.0 %collective-permute-start.9 = (f32[2,4608]{1,0:T(2,128)S(1)}, f32[2,4608]{1,0:T(2,128)S(1)}, u32[]{:S(2)}, u32[]{:S(2)}) collective-permute-start(f32[2,4608]{1,0:T(2,128)S(1)} %constant_dynamic-update-slice_fusion.3), channel_id=1, source_target_pairs={{0,2},{2,0},{4,6},{6,4},{8,10},{10,8},{12,14},{14,12},{16,18},{18,... | collective-permute-start | bytes 110600 | tf_op jit(solution)/shard_map/ppermute | solution.py:37
  371.6 55.8 %collective-permute-start.41 = (bf16[2,768,768]{2,1,0:T(8,128)(2,1)}, bf16[2,768,768]{2,1,0:T(8,128)(2,1)}, u32[]{:S(2)}, u32[]{:S(2)}) collective-permute-start(bf16[2,768,768]{2,1,0:T(8,128)(2,1)} %dynamic-slice_bitcast_fusion), channel_id=1, source_target_pairs={{0,2},{2,0},{4,6},{6,4},{8,10},{10,8},{12,14},{14,12},{16,18},{18,... | collective-permute-start | bytes 7077896 | tf_op jit(solution)/shard_map/ppermute | solution.py:37
  373.7 64.6 %collective-permute-start.32 = (bf16[2,192,3072]{2,1,0:T(8,128)(2,1)}, bf16[2,192,3072]{2,1,0:T(8,128)(2,1)}, u32[]{:S(2)}, u32[]{:S(2)}) collective-permute-start(bf16[2,192,3072]{2,1,0:T(8,128)(2,1)} %dynamic-slice_bitcast_fusion.1), channel_id=1, source_target_pairs={{0,2},{2,0},{4,6},{6,4},{8,10},{10,8},{12,14},{14,12},{16,18},{18,... | collective-permute-start | bytes 7077896 | tf_op jit(solution)/shard_map/ppermute | solution.py:37
  381.3 22.2 %collective-permute-start.14 = (bf16[2,192,2304]{2,1,0:T(8,128)(2,1)}, bf16[2,192,2304]{2,1,0:T(8,128)(2,1)}, u32[]{:S(2)}, u32[]{:S(2)}) collective-permute-start(bf16[2,192,2304]{2,1,0:T(8,128)(2,1)} %dynamic-slice_bitcast_fusion.2), channel_id=1, source_target_pairs={{0,2},{2,0},{4,6},{6,4},{8,10},{10,8},{12,14},{14,12},{16,18},{18,... | collective-permute-start | bytes 5308424 | tf_op jit(solution)/shard_map/ppermute | solution.py:37
  405.6 21.2 %collective-permute-start.15 = (bf16[192,2304]{1,0:T(8,128)(2,1)S(1)}, bf16[192,2304]{1,0:T(8,128)(2,1)S(1)}, u32[]{:S(2)}, u32[]{:S(2)}) collective-permute-start(bf16[192,2304]{1,0:T(8,128)(2,1)S(1)} %dynamic-slice_bitcast_fusion.7), channel_id=1, source_target_pairs={{0,1},{1,0},{2,3},{3,2},{4,5},{5,4},{6,7},{7,6},{8,9},{9,8},{10,11... | collective-permute-start | bytes 2654216 | tf_op jit(solution)/shard_map/ppermute | solution.py:37
  429.7 26.4 %collective-permute-start.42 = (bf16[768,768]{1,0:T(8,128)(2,1)S(1)}, bf16[768,768]{1,0:T(8,128)(2,1)S(1)}, u32[]{:S(2)}, u32[]{:S(2)}) collective-permute-start(bf16[768,768]{1,0:T(8,128)(2,1)S(1)} %dynamic-slice_bitcast_fusion.3), channel_id=1, source_target_pairs={{0,1},{1,0},{2,3},{3,2},{4,5},{5,4},{6,7},{7,6},{8,9},{9,8},{10,11... | collective-permute-start | bytes 3538952 | tf_op jit(solution)/shard_map/ppermute | solution.py:37
  444.4 37.1 %collective-permute-start.33 = (bf16[192,3072]{1,0:T(8,128)(2,1)S(1)}, bf16[192,3072]{1,0:T(8,128)(2,1)S(1)}, u32[]{:S(2)}, u32[]{:S(2)}) collective-permute-start(bf16[192,3072]{1,0:T(8,128)(2,1)S(1)} %dynamic-slice_bitcast_fusion.4), channel_id=1, source_target_pairs={{0,1},{1,0},{2,3},{3,2},{4,5},{5,4},{6,7},{7,6},{8,9},{9,8},{10,11... | collective-permute-start | bytes 3538952 | tf_op jit(solution)/shard_map/ppermute | solution.py:37
  456.5 27.1 %collective-permute-start.43 = (bf16[384,768]{1,0:T(8,128)(2,1)S(1)}, bf16[384,768]{1,0:T(8,128)(2,1)S(1)}, u32[]{:S(2)}, u32[]{:S(2)}) collective-permute-start(bf16[384,768]{1,0:T(8,128)(2,1)S(1)} %dynamic-slice_bitcast_fusion.9), channel_id=1, source_target_pairs={{0,4},{2,6},{4,0},{6,2},{8,12},{10,14},{12,8},{14,10},{16,20},{18,... | collective-permute-start | bytes 1769480 | tf_op jit(solution)/shard_map/ppermute | solution.py:37
  457.8 25.3 %collective-permute-start.20 = (bf16[48,2304]{1,0:T(8,128)(2,1)S(1)}, bf16[48,2304]{1,0:T(8,128)(2,1)S(1)}, u32[]{:S(2)}, u32[]{:S(2)}) collective-permute-start(bf16[48,2304]{1,0:T(8,128)(2,1)S(1)} %pad_maximum_fusion.27), channel_id=1, source_target_pairs={{0,8},{2,10},{4,12},{6,14},{8,0},{10,2},{12,4},{14,6},{16,24},{18,... | collective-permute-start | bytes 663560 | tf_op jit(solution)/shard_map/ppermute | solution.py:37
  483.3 21.0 %collective-permute-start.21 = (bf16[96,2304]{1,0:T(8,128)(2,1)S(1)}, bf16[96,2304]{1,0:T(8,128)(2,1)S(1)}, u32[]{:S(2)}, u32[]{:S(2)}) collective-permute-start(bf16[96,2304]{1,0:T(8,128)(2,1)S(1)} %pad_maximum_fusion.23), channel_id=1, source_target_pairs={{0,4},{2,6},{4,0},{6,2},{8,12},{10,14},{12,8},{14,10},{16,20},{18,... | collective-permute-start | bytes 1327112 | tf_op jit(solution)/shard_map/ppermute | solution.py:37
  483.8 20.6 %collective-permute-start.44 = (bf16[192,768]{1,0:T(8,128)(2,1)S(1)}, bf16[192,768]{1,0:T(8,128)(2,1)S(1)}, u32[]{:S(2)}, u32[]{:S(2)}) collective-permute-start(bf16[192,768]{1,0:T(8,128)(2,1)S(1)} %dynamic-slice_bitcast_fusion.13), channel_id=1, source_target_pairs={{0,8},{2,10},{4,12},{6,14},{8,0},{10,2},{12,4},{14,6},{16,24},{18,... | collective-permute-start | bytes 884744 | tf_op jit(solution)/shard_map/ppermute | solution.py:37
  505.5 14.8 %collective-permute-start.36 = (bf16[24,3072]{1,0:T(8,128)(2,1)S(1)}, bf16[24,3072]{1,0:T(8,128)(2,1)S(1)}, u32[]{:S(2)}, u32[]{:S(2)}) collective-permute-start(bf16[24,3072]{1,0:T(8,128)(2,1)S(1)} %dynamic-slice_bitcast_fusion.19), channel_id=1, source_target_pairs={{0,16},{2,18},{4,20},{6,22},{8,24},{10,26},{12,28},{14,30},{16,0},... | collective-permute-start | bytes 442376 | tf_op jit(solution)/shard_map/ppermute | solution.py:37
  543.6 18.5 %collective-permute-start.39 = (bf16[96,3072]{1,0:T(8,128)(2,1)S(1)}, bf16[96,3072]{1,0:T(8,128)(2,1)S(1)}, u32[]{:S(2)}, u32[]{:S(2)}) collective-permute-start(bf16[96,3072]{1,0:T(8,128)(2,1)S(1)} %pad_maximum_fusion.21), channel_id=1, source_target_pairs={{0,4},{2,6},{4,0},{6,2},{8,12},{10,14},{12,8},{14,10},{16,20},{18,... | collective-permute-start | bytes 1769480 | tf_op jit(solution)/shard_map/ppermute | solution.py:37
  544.9 21.2 %collective-permute-start.22 = (bf16[192,2304]{1,0:T(8,128)(2,1)S(1)}, bf16[192,2304]{1,0:T(8,128)(2,1)S(1)}, u32[]{:S(2)}, u32[]{:S(2)}) collective-permute-start(bf16[192,2304]{1,0:T(8,128)(2,1)S(1)} %pad_maximum_fusion.17), channel_id=1, source_target_pairs={{0,2},{2,0},{4,6},{6,4},{8,10},{10,8},{12,14},{14,12},{16,18},{18,... | collective-permute-start | bytes 2654216 | tf_op jit(solution)/shard_map/ppermute | solution.py:37
  549.8 18.7 %collective-permute-start.49 = (bf16[768,768]{1,0:T(8,128)(2,1)S(1)}, bf16[768,768]{1,0:T(8,128)(2,1)S(1)}, u32[]{:S(2)}, u32[]{:S(2)}) collective-permute-start(bf16[768,768]{1,0:T(8,128)(2,1)S(1)} %pad_maximum_fusion.16), channel_id=1, source_target_pairs={{0,2},{2,0},{4,6},{6,4},{8,10},{10,8},{12,14},{14,12},{16,18},{18,... | collective-permute-start | bytes 3538952 | tf_op jit(solution)/shard_map/ppermute | solution.py:37
  (78 other events, 946.1 us)
